TPU v7x, 32 devices: a whole 2x2x4 slice. The times are simulated.
32 devices in a mesh: space: 4 (over y, core), dir: 8 (over z, x).
Axes of the slice: x: 2, y: 2, z: 4, core: 2. Of those that a mesh axis runs over, the one named last changes fastest.
Arguments:
- multipoles: bfloat16 [2048, 256], P(('space', 'dir')), may hold values from -6 to 6
- box_scale: float32 [2048], P(('space', 'dir')), may hold values from 0.5 to 2
- fine_list: int32 [2048, 32], P(('space', 'dir')), may hold values from 0 to 2047, as said below
- wedge_index: int32 [2048, 32], P(('space', 'dir')), may hold values from 0 to 15
- list_count: int32 [2048], P(('space', 'dir')), may hold values from 16 to 32
- fine_ops: bfloat16 [16, 256, 256], replicated, may hold values from -0.1875 to 0.1875
- phases: float32 [16, 128], replicated, may hold values from -3.140625 to 3.140625
- coarse_list: int32 [16, 2048, 4], P('dir', 'space'), may hold values from 0 to 511
- coarse_ops: bfloat16 [16, 256, 256], P('dir'), may hold values from -0.1875 to 0.1875
Outputs:
- fine_local: float32 [2048, 256], P(('space', 'dir'))
- coarse_local: bfloat16 [16, 2048, 256], P(None, ('space', 'dir'))
Inputs may be any that keep to these rules, and one draw needn't show every extreme that they name: `fine_list`: each entry is the global id of a box of the same subtree as the list's box, or a box of the neighbouring subtree (one index of space up or down) held by the same index of dir; box ids run over space, then dir, then 64 boxes of a device.
All inputs are finite; a program needn't handle non-finite values.
Results may differ from a plain program's by a relative error of at most 0.018.
Values may be sent and summed in bfloat16 or wider, within the bound.
A program may use at most 64 MiB of HBM per device.

v0:
```python
import functools
import math

import jax
import jax.numpy as jnp
from jax import lax
from jax.experimental import pallas as pl
from jax.experimental.pallas import tpu as pltpu
from jax.sharding import PartitionSpec as P

MESH = pl.DeviceIdType.MESH
F32 = jnp.float32
BF16 = jnp.bfloat16
LANES = 128
HALF_TURN_HI = 3.140625
HALF_TURN_LO = 9.67653589793e-4
SINE = (1.0, -0.1666666716337204, 0.008333330973982811, -0.00019840856839437038,
        2.752503405645257e-06, -2.388494557692411e-08)
COSINE = (1.0, -0.5, 0.0416666679084301, -0.0013888884568586946, 2.4801034669508226e-05,
          -2.7524427537174332e-07, 1.9903911852026113e-09)


def horner(terms, x):
    total = jnp.full_like(x, terms[-1])
    for term in terms[-2::-1]:
        total = total * x + term
    return total


def signed_turn(angle):
    turns = jnp.floor(angle * (1.0 / math.pi) + 0.5)
    rest = (angle - turns * HALF_TURN_HI) - turns * HALF_TURN_LO
    halves = turns * 0.5
    sign = 1.0 - 4.0 * (halves - jnp.floor(halves))
    square = rest * rest
    return sign, horner(COSINE, square), horner(SINE, square) * rest


def partner(me, k):
    bit, other = 1, me
    while bit <= k:
        if k & bit:
            other = other + bit * (1 - 2 * ((me // bit) % 2))
        bit *= 2
    return other


def kernel(n_dir, n_space, boxes, dirs, block_boxes, mult, scale, lists, fine_list, wedge_index, list_count, phases,
           fine_ops, coarse_ops,
           fine_out, coarse_out,
           cand, scales, lists_v, fine_v, wedge_v, count_v, slots_v, phases_v, fine_ops_v, coarse_ops_v,
           columns, counts, weights, rotated, sums, translated,
           local_sem, rows_send, rows_recv, scale_send, scale_recv, halo_send, halo_recv, back_send, back_recv):
    me = lax.axis_index("dir")
    space = lax.axis_index("space")
    group = n_dir * boxes
    width = mult.shape[1] // 2
    terms = lists.shape[1]
    wedges = fine_ops.shape[0]
    own = pl.ds(pl.multiple_of(me * boxes, boxes), boxes)
    above = lax.rem(space + 1, n_space)
    below = lax.rem(space + n_space - 1, n_space)

    barrier = pltpu.get_barrier_semaphore()
    for k in range(1, n_dir):
        pl.semaphore_signal(barrier, inc=1, device_id={"dir": partner(me, k)}, device_id_type=MESH)
    for other in (above, below):
        pl.semaphore_signal(barrier, inc=1, device_id={"space": other}, device_id_type=MESH)

    pulls = [
        pltpu.make_async_copy(lists, lists_v, local_sem.at[0]),
        pltpu.make_async_copy(fine_list, fine_v, local_sem.at[1]),
        pltpu.make_async_copy(wedge_index, wedge_v, local_sem.at[2]),
        pltpu.make_async_copy(mult, cand.at[own], local_sem.at[3]),
        pltpu.make_async_copy(scale, scales.at[me], local_sem.at[4]),
        pltpu.make_async_copy(phases, phases_v, local_sem.at[5]),
        pltpu.make_async_copy(coarse_ops, coarse_ops_v, local_sem.at[6]),
        pltpu.make_async_copy(fine_ops, fine_ops_v, local_sem.at[7]),
        pltpu.make_async_copy(list_count, count_v, local_sem.at[8]),
    ]
    for pull in pulls:
        pull.start()

    pulls[0].wait()
    columns[...] = jnp.transpose(
        jnp.concatenate([lists_v[d].astype(F32) for d in range(dirs)], axis=0))

    pl.semaphore_wait(barrier, n_dir - 1 + 2)

    row_copies, scale_copies = {}, {}
    for k in range(n_dir - 1, 0, -1):
        to = {"dir": partner(me, k)}
        scale_copies[k] = pltpu.make_async_remote_copy(
            scale, scales.at[me], scale_send.at[k], scale_recv.at[k], device_id=to, device_id_type=MESH)
        scale_copies[k].start()
        if k == 1 or k % 2 == 0:
            row_copies[k] = pltpu.make_async_remote_copy(
                mult, cand.at[own], rows_send.at[k], rows_recv.at[k], device_id=to, device_id_type=MESH)
            row_copies[k].start()
    halos = []
    for side, other in ((0, above), (1, below)):
        halos.append(pltpu.make_async_remote_copy(
            mult, cand.at[pl.ds(group + side * boxes, boxes)], halo_send.at[side], halo_recv.at[side],
            device_id={"space": other}, device_id_type=MESH))
        halos[-1].start()

    def count_rows(i, carry):
        rows = pl.ds(pl.multiple_of(i * boxes, boxes), boxes)
        ids = columns[rows, :]
        lane = lax.broadcasted_iota(jnp.int32, (boxes, group), 1).astype(F32)
        for d in range(dirs):
            total = jnp.zeros((boxes, group), F32)
            for k in range(terms):
                at = d * terms + k
                total = total + jnp.where(ids[:, at:at + 1] == lane, 1.0, 0.0)
            counts[d, rows, :] = total.astype(BF16)
        return carry

    lax.fori_loop(0, n_dir, count_rows, 0)

    pulls[1].wait()
    pulls[2].wait()
    pulls[8].wait()
    blocks = boxes // block_boxes
    members = block_boxes * wedges
    width_list = fine_v.shape[0]
    first = fine_v[...] - space * group
    slot_values = jnp.where(
        first < 0, first + (2 * group - me * boxes), jnp.where(first < group, first, first + (boxes - me * boxes)))
    box = lax.broadcasted_iota(jnp.int32, (width_list, boxes), 1)
    term = lax.broadcasted_iota(jnp.int32, (width_list, boxes), 0)
    code_values = jnp.where(term < count_v[...], wedge_v[...] * block_boxes + box % block_boxes, -1)
    packs = LANES // block_boxes
    depth = width_list // packs
    blank = jnp.zeros((width_list, LANES - boxes), jnp.int32)
    slots_v[0] = jnp.concatenate([slot_values, blank], axis=1)
    slots_v[1] = jnp.concatenate([code_values, blank], axis=1)
    pack = lax.broadcasted_iota(jnp.int32, (depth, LANES), 1) // block_boxes

    def cells_of(which, g):
        row = jnp.zeros((depth, LANES), jnp.int32)
        for p in range(packs):
            row = jnp.where(pack == (g + p) % packs, turned[which][p], row)
        if g:
            row = pltpu.roll(row, LANES - g * block_boxes, 1)
        return jnp.concatenate([row[t:t + 1, :] for t in range(depth)], axis=1)

    turned = []
    for which in range(2):
        pieces = [slots_v[which, p * depth:(p + 1) * depth, :] for p in range(packs)]
        turned.append([pieces[0]] + [pltpu.roll(pieces[p], p * block_boxes, 1) for p in range(1, packs)])
    cells = depth * LANES
    for g in range(blocks):
        member = lax.broadcasted_iota(jnp.int32, (members, cells), 0)
        mask = jnp.where(member == cells_of(1, g), 1.0, 0.0).astype(BF16)
        candidate = lax.broadcasted_iota(jnp.int32, (cand.shape[0], cells), 0)
        onehot = jnp.where(candidate == cells_of(0, g), 1.0, 0.0).astype(BF16)
        weights[g * members:(g + 1) * members, :] = lax.dot_general(
            mask, onehot, (((1,), (1,)), ((), ())), preferred_element_type=F32).astype(BF16)

    pulls[3].wait()
    pulls[4].wait()
    pulls[5].wait()
    for k in [0, 1] + list(range(2, n_dir, 2)) + list(range(3, n_dir, 2)):
        source = partner(me, k)
        rows = pl.ds(pl.multiple_of(source * boxes, boxes), boxes)
        if k:
            scale_copies[k].wait_recv()
            row_copies[k].wait_recv()
        if k and k % 2 == 0:
            row_copies[k + 1] = pltpu.make_async_remote_copy(
                cand.at[rows], cand.at[rows], rows_send.at[k + 1], rows_recv.at[k + 1],
                device_id={"dir": partner(me, 1)}, device_id_type=MESH)
            row_copies[k + 1].start()
        column = jnp.transpose(jnp.broadcast_to(scales[source], (8, boxes)))[:, 0:1]
        picked = cand[rows, :].astype(F32)
        real, imag = picked[:, :width], picked[:, width:]
        for d in range(dirs):
            angle = phases_v[pl.ds(me * dirs + d, 1), :] * column
            sign, cosine, sine = signed_turn(angle)
            cosine, sine = cosine * sign, sine * sign
            rotated[d, rows, :width] = (real * cosine - imag * sine).astype(BF16)
            rotated[d, rows, width:] = (real * sine + imag * cosine).astype(BF16)

    pulls[6].wait()
    backs = {}
    here = coarse_out.at[pl.ds(me * dirs, dirs)]
    for pair in range(n_dir - 2, -1, -2):
        first_box = pl.multiple_of(partner(me, pair) // 2 * 2 * boxes, 2 * boxes)
        for d in range(dirs):
            gathered = jnp.dot(
                counts[d, pl.ds(first_box, 2 * boxes), :], rotated[d], preferred_element_type=F32).astype(BF16)
            result = jnp.dot(gathered, coarse_ops_v[d], preferred_element_type=F32).astype(BF16)
            for piece in range(2):
                translated[first_box // boxes + piece, d] = result[piece * boxes:(piece + 1) * boxes]
        for k in (pair + 1, pair):
            if k == 0:
                keep = pltpu.make_async_copy(translated.at[me], here, local_sem.at[0])
                keep.start()
            else:
                to = partner(me, k)
                backs[k] = pltpu.make_async_remote_copy(
                    translated.at[to], here, back_send.at[k], back_recv.at[k],
                    device_id={"dir": to}, device_id_type=MESH)
                backs[k].start()

    for halo in halos:
        halo.wait_recv()
    for g in range(blocks):
        total = jnp.dot(weights[g * members:(g + 1) * members, :], cand[...], preferred_element_type=F32).astype(BF16)
        for w in range(wedges):
            sums[w, g * block_boxes:(g + 1) * block_boxes, :] = total[w * block_boxes:(w + 1) * block_boxes]
    pulls[7].wait()
    local = jnp.zeros(fine_out.shape, F32)
    for w in range(wedges):
        local = local + jnp.dot(sums[w], fine_ops_v[w], preferred_element_type=F32)
    fine_out[...] = local

    keep.wait()
    for k in range(1, n_dir):
        backs[k].wait_recv()
    for k in range(1, n_dir):
        scale_copies[k].wait_send()
        row_copies[k].wait_send()
        backs[k].wait_send()
    for halo in halos:
        halo.wait_send()


def per_device(multipoles, box_scale, fine_list, wedge_index, list_count, fine_ops, phases, coarse_list, coarse_ops):
    n_dir, n_space = lax.axis_size("dir"), lax.axis_size("space")
    boxes, coeffs = multipoles.shape
    group = n_dir * boxes
    dirs, _, terms = coarse_list.shape
    wedges = fine_ops.shape[0]
    list_width = fine_list.shape[1]
    block_boxes = 16
    blocks = boxes // block_boxes
    lists = jnp.transpose(coarse_list, (0, 2, 1))

    hbm = pl.BlockSpec(memory_space=pltpu.HBM)
    members = blocks * block_boxes * wedges
    limit = (16 << 20) + 2 * dirs * group * group + 2 * members * group
    return pl.pallas_call(
        functools.partial(kernel, n_dir, n_space, boxes, dirs, block_boxes),
        out_shape=(
            jax.ShapeDtypeStruct((boxes, coeffs), F32),
            jax.ShapeDtypeStruct((n_dir * dirs, boxes, coeffs), BF16),
        ),
        in_specs=[hbm] * 9,
        out_specs=(pl.BlockSpec(memory_space=pltpu.VMEM), pl.BlockSpec(memory_space=pl.ANY)),
        scratch_shapes=[
            pltpu.VMEM((group + 2 * boxes, coeffs), BF16),
            pltpu.VMEM((n_dir, 1, boxes), F32),
            pltpu.VMEM(lists.shape, jnp.int32),
            pltpu.VMEM((list_width, boxes), jnp.int32),
            pltpu.VMEM((list_width, boxes), jnp.int32),
            pltpu.VMEM((1, boxes), jnp.int32),
            pltpu.VMEM((2, list_width, LANES), jnp.int32),
            pltpu.VMEM(phases.shape, F32),
            pltpu.VMEM(fine_ops.shape, BF16),
            pltpu.VMEM(coarse_ops.shape, BF16),
            pltpu.VMEM((group, dirs * terms), F32),
            pltpu.VMEM((dirs, group, group), BF16),
            pltpu.VMEM((members, group + 2 * boxes), BF16),
            pltpu.VMEM((dirs, group, coeffs), BF16),
            pltpu.VMEM((wedges, boxes, coeffs), BF16),
            pltpu.VMEM((n_dir, dirs, boxes, coeffs), BF16),
            pltpu.SemaphoreType.DMA((9,)),
        ] + [pltpu.SemaphoreType.DMA((n_dir,))] * 4 + [pltpu.SemaphoreType.DMA((2,))] * 2
        + [pltpu.SemaphoreType.DMA((n_dir,))] * 2,
        compiler_params=pltpu.CompilerParams(
            collective_id=0, has_side_effects=True, vmem_limit_bytes=limit),
        name="translations",
    )(*[
        pltpu.with_memory_space_constraint(value, pltpu.HBM)
        for value in (
            multipoles, box_scale.reshape(1, boxes), lists, fine_list.T, wedge_index.T, list_count.reshape(1, boxes),
            phases, fine_ops, coarse_ops)
    ])


def solution(mesh):
    return jax.shard_map(
        per_device,
        mesh=mesh,
        in_specs=(
            P(("space", "dir"), None),
            P(("space", "dir")),
            P(("space", "dir"), None),
            P(("space", "dir"), None),
            P(("space", "dir")),
            P(),
            P(),
            P("dir", "space", None),
            P("dir", None, None),
        ),
        out_specs=(P(("space", "dir"), None), P(None, ("space", "dir"), None)),
        check_vma=False,
    )
```

profile of v0, /device:TPU:0, one launch (start us, length us, event | category | flops | bytes accessed | tf_op | source)
XLA Modules:
  0.0 29.3 jit_solution(10309407273181823322)
XLA Ops:
  0.6 27.2 %translations.1 = (f32[64,256]{1,0:T(8,128)S(1)}, bf16[16,64,256]{2,1,0:T(8,128)(2,1)S(1)}) custom-call(bf16[64,256]{1,0:T(8,128)(2,1)} %mult.1, f32[1,64]{1,0:T(1,128)} %bitcast.8, s32[2,4,512]{2,1,0:T(4,128)} %bitcast.5, s32[32,64]{1,0:T(8,128)} %bitcast.6, s32[32,64]{1,0:T(8,128)} %bitcast.7, s32[1,64]{1,0:T(1,128)} %bitcast.9, f32[16,128]{1,0:T(8,128)} %phases.1, ...), custom_call_target="tpu_custom_call" | custom-call | tf_op jit(solution)/shard_map/translations/pallas_call | solution.py:244
  27.9 0.6 %copy.13 = f32[64,256]{1,0:T(8,128)} copy(f32[64,256]{1,0:T(8,128)S(1)} %get-tuple-element.4) | data formatting | bytes 131072
  28.5 0.8 %copy.14 = bf16[16,64,256]{2,1,0:T(8,128)(2,1)} copy(bf16[16,64,256]{2,1,0:T(8,128)(2,1)S(1)} %get-tuple-element.5) | data formatting | bytes 1048576
where the time goes:
time: 29.6 us; the launch traced here: 29.3 us
  Pallas kernels  27.2 us (92%)
  local copies, waits for them, and re-layouts  1.42 us (5%)
  between operations  0.64 us (2%)
    pallas_call x1, Pallas kernels, per_device(): pl.pallas_call(functools.partial(kernel, n_dir, n_space, boxes, dirs, blo...  27.2 us
    unnamed x2, local copies, waits for them, and re-layouts  1.42 us

commit v1 on v0

--- a/solution.py
+++ b/solution.py
@@ -48,27 +48,38 @@
 def kernel(n_dir, n_space, boxes, dirs, block_boxes, mult, scale, lists, fine_list, wedge_index, list_count, phases,
            fine_ops, coarse_ops,
            fine_out, coarse_out,
-           cand, scales, lists_v, fine_v, wedge_v, count_v, slots_v, phases_v, fine_ops_v, coarse_ops_v,
+           cand, scales, lists_v, far_lists, fine_v, wedge_v, count_v, slots_v, phases_v, fine_ops_v, coarse_ops_v, far_ops,
            columns, counts, weights, rotated, sums, translated,
-           local_sem, rows_send, rows_recv, scale_send, scale_recv, halo_send, halo_recv, back_send, back_recv):
+           local_sem, rows_send, rows_recv, scale_send, scale_recv, halo_send, halo_recv, list_sems, ops_send, ops_recv,
+           back_send, back_recv):
     me = lax.axis_index("dir")
     space = lax.axis_index("space")
     group = n_dir * boxes
+    half = n_dir // 2
+    inside = half * boxes
     width = mult.shape[1] // 2
     terms = lists.shape[1]
     wedges = fine_ops.shape[0]
     own = pl.ds(pl.multiple_of(me * boxes, boxes), boxes)
     above = lax.rem(space + 1, n_space)
     below = lax.rem(space + n_space - 1, n_space)
+    core = lax.rem(space, 2)
+    sibling = space + 1 - 2 * core
+    far = partner(me, half)
+    base = me // half * half
+    first_inside = pl.multiple_of(base * boxes, inside)
+    first_far = pl.multiple_of((half - base) * boxes, inside)
+    share_dirs = dirs // 2
+    share = pl.ds(core * share_dirs, share_dirs)
 
     barrier = pltpu.get_barrier_semaphore()
-    for k in range(1, n_dir):
+    for k in range(1, half + 1):
         pl.semaphore_signal(barrier, inc=1, device_id={"dir": partner(me, k)}, device_id_type=MESH)
     for other in (above, below):
         pl.semaphore_signal(barrier, inc=1, device_id={"space": other}, device_id_type=MESH)
 
     pulls = [
-        pltpu.make_async_copy(lists, lists_v, local_sem.at[0]),
+        pltpu.make_async_copy(lists.at[:, :, pl.ds(first_inside, inside)], lists_v, local_sem.at[0]),
         pltpu.make_async_copy(fine_list, fine_v, local_sem.at[1]),
         pltpu.make_async_copy(wedge_index, wedge_v, local_sem.at[2]),
         pltpu.make_async_copy(mult, cand.at[own], local_sem.at[3]),
@@ -78,45 +89,68 @@
         pltpu.make_async_copy(fine_ops, fine_ops_v, local_sem.at[7]),
         pltpu.make_async_copy(list_count, count_v, local_sem.at[8]),
     ]
-    for pull in pulls:
-        pull.start()
+    for at in (3, 4, 0, 6, 1, 2, 8, 5, 7):
+        pulls[at].start()
+
+    def set_columns(values):
+        columns[...] = jnp.transpose(
+            jnp.concatenate([values[d].astype(F32) for d in range(dirs)], axis=0))
+
+    def set_counts(first_slot):
+        def count_rows(i, carry):
+            rows = pl.ds(pl.multiple_of(i * boxes, boxes), boxes)
+            ids = columns[rows, :]
+            lane = lax.broadcasted_iota(jnp.int32, (boxes, group), 1).astype(F32)
+            for d in range(dirs):
+                total = jnp.zeros((boxes, group), F32)
+                for k in range(terms):
+                    at = d * terms + k
+                    total = total + jnp.where(ids[:, at:at + 1] == lane, 1.0, 0.0)
+                counts[first_slot + d, rows, :] = total.astype(BF16)
+            return carry
+
+        lax.fori_loop(0, half, count_rows, 0)
 
     pulls[0].wait()
-    columns[...] = jnp.transpose(
-        jnp.concatenate([lists_v[d].astype(F32) for d in range(dirs)], axis=0))
-
-    pl.semaphore_wait(barrier, n_dir - 1 + 2)
+    set_columns(lists_v)
+    pulls[3].wait()
+    pulls[4].wait()
+
+    pl.semaphore_wait(barrier, half + 2)
 
     row_copies, scale_copies = {}, {}
-    for k in range(n_dir - 1, 0, -1):
-        to = {"dir": partner(me, k)}
+
+    def send_block(k, to, source):
+        rows = pl.ds(pl.multiple_of(source * boxes, boxes), boxes)
+        row_copies[k] = pltpu.make_async_remote_copy(
+            cand.at[rows], cand.at[rows], rows_send.at[k], rows_recv.at[k],
+            device_id={"dir": partner(me, to)}, device_id_type=MESH)
+        row_copies[k].start()
         scale_copies[k] = pltpu.make_async_remote_copy(
-            scale, scales.at[me], scale_send.at[k], scale_recv.at[k], device_id=to, device_id_type=MESH)
+            scales.at[source], scales.at[source], scale_send.at[k], scale_recv.at[k],
+            device_id={"dir": partner(me, to)}, device_id_type=MESH)
         scale_copies[k].start()
-        if k == 1 or k % 2 == 0:
-            row_copies[k] = pltpu.make_async_remote_copy(
-                mult, cand.at[own], rows_send.at[k], rows_recv.at[k], device_id=to, device_id_type=MESH)
-            row_copies[k].start()
+
+    send_block(half, half, me)
+    for k in range(half - 1, 0, -1):
+        send_block(k, k, me)
+    list_copy = pltpu.make_async_remote_copy(
+        lists.at[:, :, pl.ds(first_far, inside)], far_lists, list_sems.at[0], list_sems.at[1],
+        device_id={"dir": far}, device_id_type=MESH)
+    list_copy.start()
     halos = []
     for side, other in ((0, above), (1, below)):
         halos.append(pltpu.make_async_remote_copy(
-            mult, cand.at[pl.ds(group + side * boxes, boxes)], halo_send.at[side], halo_recv.at[side],
+            cand.at[own], cand.at[pl.ds(group + side * boxes, boxes)], halo_send.at[side], halo_recv.at[side],
             device_id={"space": other}, device_id_type=MESH))
         halos[-1].start()
-
-    def count_rows(i, carry):
-        rows = pl.ds(pl.multiple_of(i * boxes, boxes), boxes)
-        ids = columns[rows, :]
-        lane = lax.broadcasted_iota(jnp.int32, (boxes, group), 1).astype(F32)
-        for d in range(dirs):
-            total = jnp.zeros((boxes, group), F32)
-            for k in range(terms):
-                at = d * terms + k
-                total = total + jnp.where(ids[:, at:at + 1] == lane, 1.0, 0.0)
-            counts[d, rows, :] = total.astype(BF16)
-        return carry
-
-    lax.fori_loop(0, n_dir, count_rows, 0)
+    pulls[6].wait()
+    ops_copies = [pltpu.make_async_remote_copy(
+        coarse_ops_v.at[share], far_ops.at[share], ops_send.at[0], ops_recv.at[0],
+        device_id={"dir": far}, device_id_type=MESH)]
+    ops_copies[0].start()
+
+    set_counts(0)
 
     pulls[1].wait()
     pulls[2].wait()
@@ -158,51 +192,73 @@
         weights[g * members:(g + 1) * members, :] = lax.dot_general(
             mask, onehot, (((1,), (1,)), ((), ())), preferred_element_type=F32).astype(BF16)
 
-    pulls[3].wait()
-    pulls[4].wait()
     pulls[5].wait()
-    for k in [0, 1] + list(range(2, n_dir, 2)) + list(range(3, n_dir, 2)):
-        source = partner(me, k)
+
+    def rotate(source):
         rows = pl.ds(pl.multiple_of(source * boxes, boxes), boxes)
-        if k:
-            scale_copies[k].wait_recv()
-            row_copies[k].wait_recv()
-        if k and k % 2 == 0:
-            row_copies[k + 1] = pltpu.make_async_remote_copy(
-                cand.at[rows], cand.at[rows], rows_send.at[k + 1], rows_recv.at[k + 1],
-                device_id={"dir": partner(me, 1)}, device_id_type=MESH)
-            row_copies[k + 1].start()
         column = jnp.transpose(jnp.broadcast_to(scales[source], (8, boxes)))[:, 0:1]
         picked = cand[rows, :].astype(F32)
         real, imag = picked[:, :width], picked[:, width:]
-        for d in range(dirs):
-            angle = phases_v[pl.ds(me * dirs + d, 1), :] * column
+        for slot in range(2 * dirs):
+            owner = me if slot < dirs else far
+            angle = phases_v[pl.ds(owner * dirs + slot % dirs, 1), :] * column
             sign, cosine, sine = signed_turn(angle)
             cosine, sine = cosine * sign, sine * sign
-            rotated[d, rows, :width] = (real * cosine - imag * sine).astype(BF16)
-            rotated[d, rows, width:] = (real * sine + imag * cosine).astype(BF16)
-
-    pulls[6].wait()
-    backs = {}
-    here = coarse_out.at[pl.ds(me * dirs, dirs)]
-    for pair in range(n_dir - 2, -1, -2):
-        first_box = pl.multiple_of(partner(me, pair) // 2 * 2 * boxes, 2 * boxes)
-        for d in range(dirs):
-            gathered = jnp.dot(
-                counts[d, pl.ds(first_box, 2 * boxes), :], rotated[d], preferred_element_type=F32).astype(BF16)
-            result = jnp.dot(gathered, coarse_ops_v[d], preferred_element_type=F32).astype(BF16)
-            for piece in range(2):
-                translated[first_box // boxes + piece, d] = result[piece * boxes:(piece + 1) * boxes]
-        for k in (pair + 1, pair):
-            if k == 0:
-                keep = pltpu.make_async_copy(translated.at[me], here, local_sem.at[0])
-                keep.start()
-            else:
-                to = partner(me, k)
-                backs[k] = pltpu.make_async_remote_copy(
-                    translated.at[to], here, back_send.at[k], back_recv.at[k],
-                    device_id={"dir": to}, device_id_type=MESH)
-                backs[k].start()
+            rotated[slot, rows, :width] = (real * cosine - imag * sine).astype(BF16)
+            rotated[slot, rows, width:] = (real * sine + imag * cosine).astype(BF16)
+
+    def arrived(k):
+        row_copies[k].wait_recv()
+        scale_copies[k].wait_recv()
+
+    rotate(me)
+    arrived(1)
+    rotate(partner(me, 1))
+    arrived(half)
+    for k in range(half - 1, 0, -1):
+        send_block(half + k, k, far)
+    for k in range(2, half):
+        arrived(k)
+        rotate(partner(me, k))
+    rotate(far)
+    list_copy.wait_recv()
+    set_columns(far_lists)
+    set_counts(dirs)
+    for k in range(half + 1, n_dir):
+        arrived(k)
+        rotate(partner(me, k))
+
+    backs, keeps = [], []
+
+    def translate(slot, d, at, matrix, owner):
+        gathered = jnp.dot(counts[at], rotated[at], preferred_element_type=F32).astype(BF16)
+        result = jnp.dot(gathered, matrix, preferred_element_type=F32).astype(BF16)
+        for member in range(half):
+            translated[slot, member] = result[member * boxes:(member + 1) * boxes]
+        here = coarse_out.at[owner * dirs + d]
+        for k in range(half - 1, 0, -1):
+            to = partner(me, k)
+            backs.append(pltpu.make_async_remote_copy(
+                translated.at[slot, to - base], here, back_send.at[slot, k], back_recv.at[slot, k],
+                device_id={"dir": to}, device_id_type=MESH))
+            backs[-1].start()
+        keeps.append(pltpu.make_async_copy(translated.at[slot, me - base], here, back_recv.at[slot, 0]))
+        keeps[-1].start()
+
+    for d in range(dirs):
+        translate(d, d, d, coarse_ops_v[d], me)
+    ops_copies[0].wait_recv()
+    ops_copies.append(pltpu.make_async_remote_copy(
+        far_ops.at[share], far_ops.at[share], ops_send.at[1], ops_recv.at[1],
+        device_id={"space": sibling}, device_id_type=MESH))
+    ops_copies[1].start()
+    for i in range(share_dirs):
+        d = core * share_dirs + i
+        translate(dirs + i, d, dirs + d, far_ops[d], far)
+    ops_copies[1].wait_recv()
+    for i in range(share_dirs):
+        d = (1 - core) * share_dirs + i
+        translate(dirs + share_dirs + i, d, dirs + d, far_ops[d], far)
 
     for halo in halos:
         halo.wait_recv()
@@ -216,21 +272,23 @@
         local = local + jnp.dot(sums[w], fine_ops_v[w], preferred_element_type=F32)
     fine_out[...] = local
 
-    keep.wait()
-    for k in range(1, n_dir):
-        backs[k].wait_recv()
+    for keep in keeps:
+        keep.wait()
+    for back in backs:
+        back.wait_recv()
     for k in range(1, n_dir):
         scale_copies[k].wait_send()
         row_copies[k].wait_send()
-        backs[k].wait_send()
-    for halo in halos:
-        halo.wait_send()
+    for sent in backs + halos + ops_copies + [list_copy]:
+        sent.wait_send()
 
 
 def per_device(multipoles, box_scale, fine_list, wedge_index, list_count, fine_ops, phases, coarse_list, coarse_ops):
     n_dir, n_space = lax.axis_size("dir"), lax.axis_size("space")
     boxes, coeffs = multipoles.shape
     group = n_dir * boxes
+    half = n_dir // 2
+    inside = half * boxes
     dirs, _, terms = coarse_list.shape
     wedges = fine_ops.shape[0]
     list_width = fine_list.shape[1]
@@ -240,7 +298,7 @@
 
     hbm = pl.BlockSpec(memory_space=pltpu.HBM)
     members = blocks * block_boxes * wedges
-    limit = (16 << 20) + 2 * dirs * group * group + 2 * members * group
+    limit = (20 << 20) + 4 * dirs * inside * group + 2 * members * group
     return pl.pallas_call(
         functools.partial(kernel, n_dir, n_space, boxes, dirs, block_boxes),
         out_shape=(
@@ -252,7 +310,8 @@
         scratch_shapes=[
             pltpu.VMEM((group + 2 * boxes, coeffs), BF16),
             pltpu.VMEM((n_dir, 1, boxes), F32),
-            pltpu.VMEM(lists.shape, jnp.int32),
+            pltpu.VMEM((dirs, terms, inside), jnp.int32),
+            pltpu.VMEM((dirs, terms, inside), jnp.int32),
             pltpu.VMEM((list_width, boxes), jnp.int32),
             pltpu.VMEM((list_width, boxes), jnp.int32),
             pltpu.VMEM((1, boxes), jnp.int32),
@@ -260,15 +319,16 @@
             pltpu.VMEM(phases.shape, F32),
             pltpu.VMEM(fine_ops.shape, BF16),
             pltpu.VMEM(coarse_ops.shape, BF16),
-            pltpu.VMEM((group, dirs * terms), F32),
-            pltpu.VMEM((dirs, group, group), BF16),
+            pltpu.VMEM(coarse_ops.shape, BF16),
+            pltpu.VMEM((inside, dirs * terms), F32),
+            pltpu.VMEM((2 * dirs, inside, group), BF16),
             pltpu.VMEM((members, group + 2 * boxes), BF16),
-            pltpu.VMEM((dirs, group, coeffs), BF16),
+            pltpu.VMEM((2 * dirs, group, coeffs), BF16),
             pltpu.VMEM((wedges, boxes, coeffs), BF16),
-            pltpu.VMEM((n_dir, dirs, boxes, coeffs), BF16),
+            pltpu.VMEM((2 * dirs, half, boxes, coeffs), BF16),
             pltpu.SemaphoreType.DMA((9,)),
-        ] + [pltpu.SemaphoreType.DMA((n_dir,))] * 4 + [pltpu.SemaphoreType.DMA((2,))] * 2
-        + [pltpu.SemaphoreType.DMA((n_dir,))] * 2,
+        ] + [pltpu.SemaphoreType.DMA((n_dir,))] * 4 + [pltpu.SemaphoreType.DMA((2,))] * 5
+        + [pltpu.SemaphoreType.DMA((2 * dirs, half))] * 2,
         compiler_params=pltpu.CompilerParams(
             collective_id=0, has_side_effects=True, vmem_limit_bytes=limit),
         name="translations",

time: 29.6 us -> 24 us (0.81)
  the two profiles are of different devices: /device:TPU:0 before, /device:TPU:4 now
where the time goes in v1:
time: 24 us; the launch traced here: 23.9 us
  Pallas kernels  21.8 us (91%)
  local copies, waits for them, and re-layouts  1.42 us (6%)
  between operations  0.64 us (3%)
    pallas_call x1, Pallas kernels, per_device(): pl.pallas_call(functools.partial(kernel, n_dir, n_space, boxes, dirs, blo...  21.8 us
    unnamed x2, local copies, waits for them, and re-layouts  1.42 us

profile of v1, /device:TPU:4, one launch (start us, length us, event | category | flops | bytes accessed | tf_op | source)
XLA Modules:
  0.0 23.9 jit_solution(1056897037262532266)
XLA Ops:
  0.6 21.8 %translations.1 = (f32[64,256]{1,0:T(8,128)S(1)}, bf16[16,64,256]{2,1,0:T(8,128)(2,1)S(1)}) custom-call(bf16[64,256]{1,0:T(8,128)(2,1)} %mult.1, f32[1,64]{1,0:T(1,128)} %bitcast.8, s32[2,4,512]{2,1,0:T(4,128)} %bitcast.5, s32[32,64]{1,0:T(8,128)} %bitcast.6, s32[32,64]{1,0:T(8,128)} %bitcast.7, s32[1,64]{1,0:T(1,128)} %bitcast.9, f32[16,128]{1,0:T(8,128)} %phases.1, ...), custom_call_target="tpu_custom_call" | custom-call | tf_op jit(solution)/shard_map/translations/pallas_call | solution.py:302
  22.4 0.6 %copy.13 = f32[64,256]{1,0:T(8,128)} copy(f32[64,256]{1,0:T(8,128)S(1)} %get-tuple-element.4) | data formatting | bytes 131072
  23.1 0.8 %copy.14 = bf16[16,64,256]{2,1,0:T(8,128)(2,1)} copy(bf16[16,64,256]{2,1,0:T(8,128)(2,1)S(1)} %get-tuple-element.5) | data formatting | bytes 1048576

commit v2 on v1

--- a/solution.py
+++ b/solution.py
@@ -49,9 +49,9 @@
            fine_ops, coarse_ops,
            fine_out, coarse_out,
            cand, scales, lists_v, far_lists, fine_v, wedge_v, count_v, slots_v, phases_v, fine_ops_v, coarse_ops_v, far_ops,
-           columns, counts, weights, rotated, sums, translated,
-           local_sem, rows_send, rows_recv, scale_send, scale_recv, halo_send, halo_recv, list_sems, ops_send, ops_recv,
-           back_send, back_recv):
+           columns, counts, weights, turns, rotated, sums, translated, fine_v_out,
+           local_sem, rows_send, rows_recv, scale_send, scale_recv, halo_recv, list_sems, ops_send, ops_recv,
+           back_sems):
     me = lax.axis_index("dir")
     space = lax.axis_index("space")
     group = n_dir * boxes
@@ -111,45 +111,45 @@
 
         lax.fori_loop(0, half, count_rows, 0)
 
-    pulls[0].wait()
-    set_columns(lists_v)
-    pulls[3].wait()
-    pulls[4].wait()
-
     pl.semaphore_wait(barrier, half + 2)
 
-    row_copies, scale_copies = {}, {}
-
-    def send_block(k, to, source):
-        rows = pl.ds(pl.multiple_of(source * boxes, boxes), boxes)
-        row_copies[k] = pltpu.make_async_remote_copy(
-            cand.at[rows], cand.at[rows], rows_send.at[k], rows_recv.at[k],
-            device_id={"dir": partner(me, to)}, device_id_type=MESH)
-        row_copies[k].start()
-        scale_copies[k] = pltpu.make_async_remote_copy(
-            scales.at[source], scales.at[source], scale_send.at[k], scale_recv.at[k],
-            device_id={"dir": partner(me, to)}, device_id_type=MESH)
-        scale_copies[k].start()
-
-    send_block(half, half, me)
-    for k in range(half - 1, 0, -1):
-        send_block(k, k, me)
+    def rows_of(source):
+        return pl.ds(pl.multiple_of(source * boxes, boxes), boxes)
+
+    def stage(k):
+        return 0 if k < half else 1 if k == half else 2
+
+    def rows_wait(blocks, sem):
+        data = cand.at[pl.ds(0, blocks * boxes)]
+        pltpu.make_async_copy(data, data, sem).wait()
+
+    def scales_wait(blocks, sem):
+        data = scales.at[pl.ds(0, blocks)]
+        pltpu.make_async_copy(data, data, sem).wait()
+
+    def send_rows(k, to, data, source):
+        pltpu.make_async_remote_copy(
+            data, cand.at[rows_of(source)], rows_send.at[0], rows_recv.at[stage(k)],
+            device_id={"dir": partner(me, to)}, device_id_type=MESH).start()
+
+    def send_scale(k, to, data, source):
+        pltpu.make_async_remote_copy(
+            data, scales.at[source], scale_send.at[0], scale_recv.at[stage(k)],
+            device_id={"dir": partner(me, to)}, device_id_type=MESH).start()
+
+    for k in range(half, 0, -1):
+        send_scale(k, k, scale, me)
+        send_rows(k, k, mult, me)
+    for side, other in ((0, above), (1, below)):
+        pltpu.make_async_remote_copy(
+            mult, cand.at[pl.ds(group + side * boxes, boxes)], rows_send.at[0], halo_recv.at[0],
+            device_id={"space": other}, device_id_type=MESH).start()
     list_copy = pltpu.make_async_remote_copy(
         lists.at[:, :, pl.ds(first_far, inside)], far_lists, list_sems.at[0], list_sems.at[1],
         device_id={"dir": far}, device_id_type=MESH)
     list_copy.start()
-    halos = []
-    for side, other in ((0, above), (1, below)):
-        halos.append(pltpu.make_async_remote_copy(
-            cand.at[own], cand.at[pl.ds(group + side * boxes, boxes)], halo_send.at[side], halo_recv.at[side],
-            device_id={"space": other}, device_id_type=MESH))
-        halos[-1].start()
-    pulls[6].wait()
-    ops_copies = [pltpu.make_async_remote_copy(
-        coarse_ops_v.at[share], far_ops.at[share], ops_send.at[0], ops_recv.at[0],
-        device_id={"dir": far}, device_id_type=MESH)]
-    ops_copies[0].start()
-
+    pulls[0].wait()
+    set_columns(lists_v)
     set_counts(0)
 
     pulls[1].wait()
@@ -192,43 +192,58 @@
         weights[g * members:(g + 1) * members, :] = lax.dot_general(
             mask, onehot, (((1,), (1,)), ((), ())), preferred_element_type=F32).astype(BF16)
 
-    pulls[5].wait()
-
-    def rotate(source):
-        rows = pl.ds(pl.multiple_of(source * boxes, boxes), boxes)
+    def angles(source):
         column = jnp.transpose(jnp.broadcast_to(scales[source], (8, boxes)))[:, 0:1]
-        picked = cand[rows, :].astype(F32)
-        real, imag = picked[:, :width], picked[:, width:]
         for slot in range(2 * dirs):
             owner = me if slot < dirs else far
             angle = phases_v[pl.ds(owner * dirs + slot % dirs, 1), :] * column
             sign, cosine, sine = signed_turn(angle)
-            cosine, sine = cosine * sign, sine * sign
+            turns[slot, rows_of(source), :width] = cosine * sign
+            turns[slot, rows_of(source), width:] = sine * sign
+
+    def rotate(source):
+        rows = rows_of(source)
+        picked = cand[rows, :].astype(F32)
+        real, imag = picked[:, :width], picked[:, width:]
+        for slot in range(2 * dirs):
+            cosine, sine = turns[slot, rows, :width], turns[slot, rows, width:]
             rotated[slot, rows, :width] = (real * cosine - imag * sine).astype(BF16)
             rotated[slot, rows, width:] = (real * sine + imag * cosine).astype(BF16)
 
-    def arrived(k):
-        row_copies[k].wait_recv()
-        scale_copies[k].wait_recv()
-
+    pulls[3].wait()
+    pulls[4].wait()
+    pulls[5].wait()
+    angles(me)
     rotate(me)
-    arrived(1)
-    rotate(partner(me, 1))
-    arrived(half)
+    scales_wait(1, scale_recv.at[1])
     for k in range(half - 1, 0, -1):
-        send_block(half + k, k, far)
-    for k in range(2, half):
-        arrived(k)
+        send_scale(half + k, k, scales.at[far], far)
+    rows_wait(1, rows_recv.at[1])
+    for k in range(half - 1, 0, -1):
+        send_rows(half + k, k, cand.at[rows_of(far)], far)
+    pulls[6].wait()
+    ops_copies = [pltpu.make_async_remote_copy(
+        coarse_ops_v.at[share], far_ops.at[share], ops_send.at[0], ops_recv.at[0],
+        device_id={"dir": far}, device_id_type=MESH)]
+    ops_copies[0].start()
+
+    angles(far)
+    scales_wait(half - 1, scale_recv.at[0])
+    for k in range(1, half):
+        angles(partner(me, k))
+    rotate(far)
+    rows_wait(half - 1, rows_recv.at[0])
+    for k in range(1, half):
         rotate(partner(me, k))
-    rotate(far)
     list_copy.wait_recv()
     set_columns(far_lists)
     set_counts(dirs)
+    scales_wait(half - 1, scale_recv.at[2])
     for k in range(half + 1, n_dir):
-        arrived(k)
+        angles(partner(me, k))
+    rows_wait(half - 1, rows_recv.at[2])
+    for k in range(half + 1, n_dir):
         rotate(partner(me, k))
-
-    backs, keeps = [], []
 
     def translate(slot, d, at, matrix, owner):
         gathered = jnp.dot(counts[at], rotated[at], preferred_element_type=F32).astype(BF16)
@@ -238,12 +253,10 @@
         here = coarse_out.at[owner * dirs + d]
         for k in range(half - 1, 0, -1):
             to = partner(me, k)
-            backs.append(pltpu.make_async_remote_copy(
-                translated.at[slot, to - base], here, back_send.at[slot, k], back_recv.at[slot, k],
-                device_id={"dir": to}, device_id_type=MESH))
-            backs[-1].start()
-        keeps.append(pltpu.make_async_copy(translated.at[slot, me - base], here, back_recv.at[slot, 0]))
-        keeps[-1].start()
+            pltpu.make_async_remote_copy(
+                translated.at[slot, to - base], here, back_sems.at[0], back_sems.at[1],
+                device_id={"dir": to}, device_id_type=MESH).start()
+        pltpu.make_async_copy(translated.at[slot, me - base], here, back_sems.at[2]).start()
 
     for d in range(dirs):
         translate(d, d, d, coarse_ops_v[d], me)
@@ -260,27 +273,40 @@
         d = (1 - core) * share_dirs + i
         translate(dirs + share_dirs + i, d, dirs + d, far_ops[d], far)
 
-    for halo in halos:
-        halo.wait_recv()
+    rows_wait(2, halo_recv.at[0])
     for g in range(blocks):
         total = jnp.dot(weights[g * members:(g + 1) * members, :], cand[...], preferred_element_type=F32).astype(BF16)
         for w in range(wedges):
             sums[w, g * block_boxes:(g + 1) * block_boxes, :] = total[w * block_boxes:(w + 1) * block_boxes]
     pulls[7].wait()
-    local = jnp.zeros(fine_out.shape, F32)
+    local = jnp.zeros(fine_v_out.shape, F32)
     for w in range(wedges):
         local = local + jnp.dot(sums[w], fine_ops_v[w], preferred_element_type=F32)
-    fine_out[...] = local
-
-    for keep in keeps:
-        keep.wait()
-    for back in backs:
-        back.wait_recv()
-    for k in range(1, n_dir):
-        scale_copies[k].wait_send()
-        row_copies[k].wait_send()
-    for sent in backs + halos + ops_copies + [list_copy]:
+    fine_v_out[...] = local
+    fine_copy = pltpu.make_async_copy(fine_v_out, fine_out, local_sem.at[0])
+    fine_copy.start()
+
+    fine_copy.wait()
+    kept = translated.at[:, pl.ds(0, 1)]
+    pltpu.make_async_copy(kept, kept, back_sems.at[2]).wait()
+    moved = translated.at[:, pl.ds(0, half - 1)]
+    pltpu.make_async_copy(moved, moved, back_sems.at[1]).wait()
+    pltpu.make_async_copy(moved, moved, back_sems.at[0]).wait()
+    rows_wait(n_dir + 1, rows_send.at[0])
+    scales_wait(n_dir - 1, scale_send.at[0])
+    for sent in ops_copies + [list_copy]:
         sent.wait_send()
+
+
+def settle(fine_in, coarse_in, fine_out, coarse_out, sems):
+    copies = [
+        pltpu.make_async_copy(coarse_in, coarse_out, sems.at[0]),
+        pltpu.make_async_copy(fine_in, fine_out, sems.at[1]),
+    ]
+    for copy in copies:
+        copy.start()
+    for copy in copies:
+        copy.wait()
 
 
 def per_device(multipoles, box_scale, fine_list, wedge_index, list_count, fine_ops, phases, coarse_list, coarse_ops):
@@ -298,15 +324,15 @@
 
     hbm = pl.BlockSpec(memory_space=pltpu.HBM)
     members = blocks * block_boxes * wedges
-    limit = (20 << 20) + 4 * dirs * inside * group + 2 * members * group
-    return pl.pallas_call(
+    limit = (20 << 20) + 4 * dirs * group * (inside + 2 * coeffs) + 2 * members * group
+    outs = pl.pallas_call(
         functools.partial(kernel, n_dir, n_space, boxes, dirs, block_boxes),
         out_shape=(
             jax.ShapeDtypeStruct((boxes, coeffs), F32),
             jax.ShapeDtypeStruct((n_dir * dirs, boxes, coeffs), BF16),
         ),
         in_specs=[hbm] * 9,
-        out_specs=(pl.BlockSpec(memory_space=pltpu.VMEM), pl.BlockSpec(memory_space=pl.ANY)),
+        out_specs=(pl.BlockSpec(memory_space=pl.ANY), pl.BlockSpec(memory_space=pl.ANY)),
         scratch_shapes=[
             pltpu.VMEM((group + 2 * boxes, coeffs), BF16),
             pltpu.VMEM((n_dir, 1, boxes), F32),
@@ -323,12 +349,13 @@
             pltpu.VMEM((inside, dirs * terms), F32),
             pltpu.VMEM((2 * dirs, inside, group), BF16),
             pltpu.VMEM((members, group + 2 * boxes), BF16),
+            pltpu.VMEM((2 * dirs, group, coeffs), F32),
             pltpu.VMEM((2 * dirs, group, coeffs), BF16),
             pltpu.VMEM((wedges, boxes, coeffs), BF16),
             pltpu.VMEM((2 * dirs, half, boxes, coeffs), BF16),
+            pltpu.VMEM((boxes, coeffs), F32),
             pltpu.SemaphoreType.DMA((9,)),
-        ] + [pltpu.SemaphoreType.DMA((n_dir,))] * 4 + [pltpu.SemaphoreType.DMA((2,))] * 5
-        + [pltpu.SemaphoreType.DMA((2 * dirs, half))] * 2,
+        ] + [pltpu.SemaphoreType.DMA((n,)) for n in (1, 3, 1, 3, 1, 2, 2, 2, 3)],
         compiler_params=pltpu.CompilerParams(
             collective_id=0, has_side_effects=True, vmem_limit_bytes=limit),
         name="translations",
@@ -338,6 +365,14 @@
             multipoles, box_scale.reshape(1, boxes), lists, fine_list.T, wedge_index.T, list_count.reshape(1, boxes),
             phases, fine_ops, coarse_ops)
     ])
+    return pl.pallas_call(
+        settle,
+        out_shape=tuple(jax.ShapeDtypeStruct(out.shape, out.dtype) for out in outs),
+        in_specs=[pl.BlockSpec(memory_space=pltpu.VMEM)] * 2,
+        out_specs=tuple(pl.BlockSpec(memory_space=pltpu.HBM) for _ in outs),
+        scratch_shapes=[pltpu.SemaphoreType.DMA((2,))],
+        name="settle",
+    )(*[pltpu.with_memory_space_constraint(out, pltpu.VMEM) for out in outs])
 
 
 def solution(mesh):

time: 24 us -> 22.3 us (0.929)
  the two profiles are of different devices: /device:TPU:4 before, /device:TPU:0 now
where the time goes in v2:
time: 22.3 us; the launch traced here: 22.2 us
  Pallas kernels  21.5 us (96%)
  between operations  0.64 us (3%)
    pallas_call x1, Pallas kernels, per_device(): pl.pallas_call(functools.partial(kernel, n_dir, n_space, boxes, dirs, blo...  20.7 us
    pallas_call x1, Pallas kernels, per_device(): pl.pallas_call(settle, out_shape=tuple((jax.ShapeDtypeStruct(out.shape, o...  0.82 us

profile of v2, /device:TPU:0, one launch (start us, length us, event | category | flops | bytes accessed | tf_op | source)
XLA Modules:
  0.0 22.2 jit_solution(4198620360557150964)
XLA Ops:
  0.6 20.7 %translations.1 = (f32[64,256]{1,0:T(8,128)S(1)}, bf16[16,64,256]{2,1,0:T(8,128)(2,1)S(1)}) custom-call(bf16[64,256]{1,0:T(8,128)(2,1)} %mult.1, f32[1,64]{1,0:T(1,128)} %bitcast.8, s32[2,4,512]{2,1,0:T(4,128)} %bitcast.5, s32[32,64]{1,0:T(8,128)} %bitcast.6, s32[32,64]{1,0:T(8,128)} %bitcast.7, s32[1,64]{1,0:T(1,128)} %bitcast.9, f32[16,128]{1,0:T(8,128)} %phases.1, ...), custom_call_target="tpu_custom_call" | custom-call | tf_op jit(solution)/shard_map/translations/pallas_call | solution.py:328
  21.4 0.8 %settle.1 = (f32[64,256]{1,0:T(8,128)}, bf16[16,64,256]{2,1,0:T(8,128)(2,1)}) custom-call(f32[64,256]{1,0:T(8,128)S(1)} %get-tuple-element.4.fine_in, bf16[16,64,256]{2,1,0:T(8,128)(2,1)S(1)} %get-tuple-element.5.coarse_in), custom_call_target="tpu_custom_call" | custom-call | tf_op jit(solution)/shard_map/settle/pallas_call | solution.py:368

commit v3 on v2

--- a/solution.py
+++ b/solution.py
@@ -49,9 +49,9 @@
            fine_ops, coarse_ops,
            fine_out, coarse_out,
            cand, scales, lists_v, far_lists, fine_v, wedge_v, count_v, slots_v, phases_v, fine_ops_v, coarse_ops_v, far_ops,
-           columns, counts, weights, turns, rotated, sums, translated, fine_v_out,
-           local_sem, rows_send, rows_recv, scale_send, scale_recv, halo_recv, list_sems, ops_send, ops_recv,
-           back_sems):
+           columns, counts, weights, turns, rotated, sums, translated, gathered_out, gathered_in, fine_v_out,
+           local_sem, rows_send, rows_recv, scale_send, scale_recv, halo_recv, list_sems, ops_sems,
+           swap_sems, back_sems):
     me = lax.axis_index("dir")
     space = lax.axis_index("space")
     group = n_dir * boxes
@@ -70,12 +70,19 @@
     first_inside = pl.multiple_of(base * boxes, inside)
     first_far = pl.multiple_of((half - base) * boxes, inside)
     share_dirs = dirs // 2
+    level = space // 2
+    levels = n_space // 2
+    deep = coarse_ops.shape[1] // levels
+    storeys = [2 * lax.rem(level + i, levels) + core for i in range(1, levels)]
     share = pl.ds(core * share_dirs, share_dirs)
 
     barrier = pltpu.get_barrier_semaphore()
     for k in range(1, half + 1):
         pl.semaphore_signal(barrier, inc=1, device_id={"dir": partner(me, k)}, device_id_type=MESH)
-    for other in (above, below):
+    for k in range(1, half):
+        pl.semaphore_signal(
+            barrier, inc=1, device_id={"dir": partner(me, k), "space": sibling}, device_id_type=MESH)
+    for other in [above, below] + storeys:
         pl.semaphore_signal(barrier, inc=1, device_id={"space": other}, device_id_type=MESH)
 
     pulls = [
@@ -111,7 +118,7 @@
 
         lax.fori_loop(0, half, count_rows, 0)
 
-    pl.semaphore_wait(barrier, half + 2)
+    pl.semaphore_wait(barrier, 2 * half + levels)
 
     def rows_of(source):
         return pl.ds(pl.multiple_of(source * boxes, boxes), boxes)
@@ -148,9 +155,15 @@
         lists.at[:, :, pl.ds(first_far, inside)], far_lists, list_sems.at[0], list_sems.at[1],
         device_id={"dir": far}, device_id_type=MESH)
     list_copy.start()
+    deeps = pl.ds(pl.multiple_of(level * deep, deep), deep)
+    ops_copy = pltpu.make_async_remote_copy(
+        coarse_ops_v.at[share, deeps], far_ops.at[:, deeps], ops_sems.at[0], ops_sems.at[1],
+        device_id={"dir": far}, device_id_type=MESH)
+
     pulls[0].wait()
     set_columns(lists_v)
     set_counts(0)
+    pulls[6].wait()
 
     pulls[1].wait()
     pulls[2].wait()
@@ -191,6 +204,8 @@
         onehot = jnp.where(candidate == cells_of(0, g), 1.0, 0.0).astype(BF16)
         weights[g * members:(g + 1) * members, :] = lax.dot_general(
             mask, onehot, (((1,), (1,)), ((), ())), preferred_element_type=F32).astype(BF16)
+        if g == 1:
+            ops_copy.start()
 
     def angles(source):
         column = jnp.transpose(jnp.broadcast_to(scales[source], (8, boxes)))[:, 0:1]
@@ -221,12 +236,6 @@
     rows_wait(1, rows_recv.at[1])
     for k in range(half - 1, 0, -1):
         send_rows(half + k, k, cand.at[rows_of(far)], far)
-    pulls[6].wait()
-    ops_copies = [pltpu.make_async_remote_copy(
-        coarse_ops_v.at[share], far_ops.at[share], ops_send.at[0], ops_recv.at[0],
-        device_id={"dir": far}, device_id_type=MESH)]
-    ops_copies[0].start()
-
     angles(far)
     scales_wait(half - 1, scale_recv.at[0])
     for k in range(1, half):
@@ -238,6 +247,11 @@
     list_copy.wait_recv()
     set_columns(far_lists)
     set_counts(dirs)
+    ops_copy.wait_recv()
+    for other in storeys:
+        pltpu.make_async_remote_copy(
+            far_ops.at[:, deeps], far_ops.at[:, deeps], ops_sems.at[2], ops_sems.at[3],
+            device_id={"space": other}, device_id_type=MESH).start()
     scales_wait(half - 1, scale_recv.at[2])
     for k in range(half + 1, n_dir):
         angles(partner(me, k))
@@ -245,33 +259,44 @@
     for k in range(half + 1, n_dir):
         rotate(partner(me, k))
 
-    def translate(slot, d, at, matrix, owner):
-        gathered = jnp.dot(counts[at], rotated[at], preferred_element_type=F32).astype(BF16)
+    def gather(at):
+        return jnp.dot(counts[at], rotated[at], preferred_element_type=F32).astype(BF16)
+
+    def translate(gathered, matrix, slot, here, home):
         result = jnp.dot(gathered, matrix, preferred_element_type=F32).astype(BF16)
+        first = slot * half
         for member in range(half):
-            translated[slot, member] = result[member * boxes:(member + 1) * boxes]
-        here = coarse_out.at[owner * dirs + d]
-        for k in range(half - 1, 0, -1):
+            translated[first + member] = result[member * boxes:(member + 1) * boxes]
+        for k in range(half - 1, -1, -1):
             to = partner(me, k)
-            pltpu.make_async_remote_copy(
-                translated.at[slot, to - base], here, back_sems.at[0], back_sems.at[1],
-                device_id={"dir": to}, device_id_type=MESH).start()
-        pltpu.make_async_copy(translated.at[slot, me - base], here, back_sems.at[2]).start()
+            piece = translated.at[first + to - base]
+            if k or not home:
+                where = {"dir": to} if home else {"dir": to, "space": sibling}
+                pltpu.make_async_remote_copy(
+                    piece, here, back_sems.at[0], back_sems.at[1], device_id=where, device_id_type=MESH).start()
+            else:
+                pltpu.make_async_copy(piece, here, back_sems.at[2]).start()
+
+    def far_out(i):
+        return coarse_out.at[far * dirs + core * share_dirs + i]
 
     for d in range(dirs):
-        translate(d, d, d, coarse_ops_v[d], me)
-    ops_copies[0].wait_recv()
-    ops_copies.append(pltpu.make_async_remote_copy(
-        far_ops.at[share], far_ops.at[share], ops_send.at[1], ops_recv.at[1],
-        device_id={"space": sibling}, device_id_type=MESH))
-    ops_copies[1].start()
+        translate(gather(d), coarse_ops_v[d], d, coarse_out.at[me * dirs + d], True)
+        if d == 0:
+            for i in range(share_dirs):
+                gathered_out[i] = gather(dirs + (1 - core) * share_dirs + i)
+            swap = pltpu.make_async_remote_copy(
+                gathered_out, gathered_in, swap_sems.at[0], swap_sems.at[1],
+                device_id={"space": sibling}, device_id_type=MESH)
+            swap.start()
+    own_gathered = [gather(dirs + core * share_dirs + i) for i in range(share_dirs)]
+    rest = far_ops.at[:, pl.ds(0, (levels - 1) * deep)]
+    pltpu.make_async_copy(rest, rest, ops_sems.at[3]).wait()
     for i in range(share_dirs):
-        d = core * share_dirs + i
-        translate(dirs + i, d, dirs + d, far_ops[d], far)
-    ops_copies[1].wait_recv()
+        translate(own_gathered[i], far_ops[i], dirs + i, far_out(i), True)
+    swap.wait_recv()
     for i in range(share_dirs):
-        d = (1 - core) * share_dirs + i
-        translate(dirs + share_dirs + i, d, dirs + d, far_ops[d], far)
+        translate(gathered_in[i], far_ops[i], dirs + share_dirs + i, far_out(i), False)
 
     rows_wait(2, halo_recv.at[0])
     for g in range(blocks):
@@ -287,14 +312,15 @@
     fine_copy.start()
 
     fine_copy.wait()
-    kept = translated.at[:, pl.ds(0, 1)]
+    kept = translated.at[pl.ds(0, dirs + share_dirs)]
     pltpu.make_async_copy(kept, kept, back_sems.at[2]).wait()
-    moved = translated.at[:, pl.ds(0, half - 1)]
+    moved = translated.at[pl.ds(0, 2 * dirs * half - dirs - share_dirs)]
     pltpu.make_async_copy(moved, moved, back_sems.at[1]).wait()
     pltpu.make_async_copy(moved, moved, back_sems.at[0]).wait()
     rows_wait(n_dir + 1, rows_send.at[0])
     scales_wait(n_dir - 1, scale_send.at[0])
-    for sent in ops_copies + [list_copy]:
+    pltpu.make_async_copy(rest, rest, ops_sems.at[2]).wait()
+    for sent in (ops_copy, list_copy, swap):
         sent.wait_send()
 
 
@@ -345,17 +371,19 @@
             pltpu.VMEM(phases.shape, F32),
             pltpu.VMEM(fine_ops.shape, BF16),
             pltpu.VMEM(coarse_ops.shape, BF16),
-            pltpu.VMEM(coarse_ops.shape, BF16),
+            pltpu.VMEM((dirs // 2,) + coarse_ops.shape[1:], BF16),
             pltpu.VMEM((inside, dirs * terms), F32),
             pltpu.VMEM((2 * dirs, inside, group), BF16),
             pltpu.VMEM((members, group + 2 * boxes), BF16),
             pltpu.VMEM((2 * dirs, group, coeffs), F32),
             pltpu.VMEM((2 * dirs, group, coeffs), BF16),
             pltpu.VMEM((wedges, boxes, coeffs), BF16),
-            pltpu.VMEM((2 * dirs, half, boxes, coeffs), BF16),
+            pltpu.VMEM((2 * dirs * half, boxes, coeffs), BF16),
+            pltpu.VMEM((dirs // 2, inside, coeffs), BF16),
+            pltpu.VMEM((dirs // 2, inside, coeffs), BF16),
             pltpu.VMEM((boxes, coeffs), F32),
             pltpu.SemaphoreType.DMA((9,)),
-        ] + [pltpu.SemaphoreType.DMA((n,)) for n in (1, 3, 1, 3, 1, 2, 2, 2, 3)],
+        ] + [pltpu.SemaphoreType.DMA((n,)) for n in (1, 3, 1, 3, 1, 2, 4, 2, 3)],
         compiler_params=pltpu.CompilerParams(
             collective_id=0, has_side_effects=True, vmem_limit_bytes=limit),
         name="translations",

time: 22.3 us -> 21.4 us (0.960)
  Pallas kernels: 21.5 us -> 20.6 us
    pallas_call x1, Pallas kernels: 20.7 us -> 19.8 us  [per_device(): pl.pallas_call(functools.partial(kernel, n_dir, n_space, boxes, dirs, blo...]
where the time goes in v3:
time: 21.4 us; the launch traced here: 21.2 us
  Pallas kernels  20.6 us (96%)
  between operations  0.64 us (3%)
    pallas_call x1, Pallas kernels, per_device(): pl.pallas_call(functools.partial(kernel, n_dir, n_space, boxes, dirs, blo...  19.8 us
    pallas_call x1, Pallas kernels, per_device(): pl.pallas_call(settle, out_shape=tuple((jax.ShapeDtypeStruct(out.shape, o...  0.82 us

profile of v3, /device:TPU:0, one launch (start us, length us, event | category | flops | bytes accessed | tf_op | source)
XLA Modules:
  0.0 21.2 jit_solution(17170207271103238326)
XLA Ops:
  0.6 19.8 %translations.1 = (f32[64,256]{1,0:T(8,128)S(1)}, bf16[16,64,256]{2,1,0:T(8,128)(2,1)S(1)}) custom-call(bf16[64,256]{1,0:T(8,128)(2,1)} %mult.1, f32[1,64]{1,0:T(1,128)} %bitcast.8, s32[2,4,512]{2,1,0:T(4,128)} %bitcast.5, s32[32,64]{1,0:T(8,128)} %bitcast.6, s32[32,64]{1,0:T(8,128)} %bitcast.7, s32[1,64]{1,0:T(1,128)} %bitcast.9, f32[16,128]{1,0:T(8,128)} %phases.1, ...), custom_call_target="tpu_custom_call" | custom-call | tf_op jit(solution)/shard_map/translations/pallas_call | solution.py:354
  20.4 0.8 %settle.1 = (f32[64,256]{1,0:T(8,128)}, bf16[16,64,256]{2,1,0:T(8,128)(2,1)}) custom-call(f32[64,256]{1,0:T(8,128)S(1)} %get-tuple-element.4.fine_in, bf16[16,64,256]{2,1,0:T(8,128)(2,1)S(1)} %get-tuple-element.5.coarse_in), custom_call_target="tpu_custom_call" | custom-call | tf_op jit(solution)/shard_map/settle/pallas_call | solution.py:396

commit v4 on v3

--- a/solution.py
+++ b/solution.py
@@ -72,7 +72,10 @@
     share_dirs = dirs // 2
     level = space // 2
     levels = n_space // 2
-    deep = coarse_ops.shape[1] // levels
+    shared_deep = coarse_ops.shape[1] // 2
+    deep = shared_deep // levels
+    passed = pl.ds(pl.multiple_of(level * deep, deep), deep)
+    common = pl.ds(shared_deep, coarse_ops.shape[1] - shared_deep)
     storeys = [2 * lax.rem(level + i, levels) + core for i in range(1, levels)]
     share = pl.ds(core * share_dirs, share_dirs)
 
@@ -144,9 +147,11 @@
             data, scales.at[source], scale_send.at[0], scale_recv.at[stage(k)],
             device_id={"dir": partner(me, to)}, device_id_type=MESH).start()
 
+    pulls[3].wait()
+    pulls[4].wait()
     for k in range(half, 0, -1):
-        send_scale(k, k, scale, me)
-        send_rows(k, k, mult, me)
+        send_scale(k, k, scales.at[me], me)
+        send_rows(k, k, cand.at[own], me)
     for side, other in ((0, above), (1, below)):
         pltpu.make_async_remote_copy(
             mult, cand.at[pl.ds(group + side * boxes, boxes)], rows_send.at[0], halo_recv.at[0],
@@ -155,10 +160,10 @@
         lists.at[:, :, pl.ds(first_far, inside)], far_lists, list_sems.at[0], list_sems.at[1],
         device_id={"dir": far}, device_id_type=MESH)
     list_copy.start()
-    deeps = pl.ds(pl.multiple_of(level * deep, deep), deep)
-    ops_copy = pltpu.make_async_remote_copy(
-        coarse_ops_v.at[share, deeps], far_ops.at[:, deeps], ops_sems.at[0], ops_sems.at[1],
-        device_id={"dir": far}, device_id_type=MESH)
+    ops_copies = [pltpu.make_async_remote_copy(
+        coarse_ops_v.at[share, rows], far_ops.at[:, rows],
+        ops_sems.at[0], ops_sems.at[3 + at], device_id={"dir": far}, device_id_type=MESH)
+        for at, rows in enumerate((passed, common))]
 
     pulls[0].wait()
     set_columns(lists_v)
@@ -205,7 +210,8 @@
         weights[g * members:(g + 1) * members, :] = lax.dot_general(
             mask, onehot, (((1,), (1,)), ((), ())), preferred_element_type=F32).astype(BF16)
         if g == 1:
-            ops_copy.start()
+            for copy in ops_copies:
+                copy.start()
 
     def angles(source):
         column = jnp.transpose(jnp.broadcast_to(scales[source], (8, boxes)))[:, 0:1]
@@ -225,8 +231,6 @@
             rotated[slot, rows, :width] = (real * cosine - imag * sine).astype(BF16)
             rotated[slot, rows, width:] = (real * sine + imag * cosine).astype(BF16)
 
-    pulls[3].wait()
-    pulls[4].wait()
     pulls[5].wait()
     angles(me)
     rotate(me)
@@ -247,14 +251,14 @@
     list_copy.wait_recv()
     set_columns(far_lists)
     set_counts(dirs)
-    ops_copy.wait_recv()
-    for other in storeys:
-        pltpu.make_async_remote_copy(
-            far_ops.at[:, deeps], far_ops.at[:, deeps], ops_sems.at[2], ops_sems.at[3],
-            device_id={"space": other}, device_id_type=MESH).start()
     scales_wait(half - 1, scale_recv.at[2])
     for k in range(half + 1, n_dir):
         angles(partner(me, k))
+    ops_copies[0].wait_recv()
+    for other in storeys:
+        pltpu.make_async_remote_copy(
+            far_ops.at[:, passed], far_ops.at[:, passed], ops_sems.at[1], ops_sems.at[2],
+            device_id={"space": other}, device_id_type=MESH).start()
     rows_wait(half - 1, rows_recv.at[2])
     for k in range(half + 1, n_dir):
         rotate(partner(me, k))
@@ -282,16 +286,16 @@
 
     for d in range(dirs):
         translate(gather(d), coarse_ops_v[d], d, coarse_out.at[me * dirs + d], True)
-        if d == 0:
-            for i in range(share_dirs):
-                gathered_out[i] = gather(dirs + (1 - core) * share_dirs + i)
-            swap = pltpu.make_async_remote_copy(
-                gathered_out, gathered_in, swap_sems.at[0], swap_sems.at[1],
-                device_id={"space": sibling}, device_id_type=MESH)
-            swap.start()
+    for i in range(share_dirs):
+        gathered_out[i] = gather(dirs + (1 - core) * share_dirs + i)
+    swap = pltpu.make_async_remote_copy(
+        gathered_out, gathered_in, swap_sems.at[0], swap_sems.at[1],
+        device_id={"space": sibling}, device_id_type=MESH)
+    swap.start()
     own_gathered = [gather(dirs + core * share_dirs + i) for i in range(share_dirs)]
     rest = far_ops.at[:, pl.ds(0, (levels - 1) * deep)]
-    pltpu.make_async_copy(rest, rest, ops_sems.at[3]).wait()
+    pltpu.make_async_copy(rest, rest, ops_sems.at[2]).wait()
+    ops_copies[1].wait_recv()
     for i in range(share_dirs):
         translate(own_gathered[i], far_ops[i], dirs + i, far_out(i), True)
     swap.wait_recv()
@@ -319,8 +323,10 @@
     pltpu.make_async_copy(moved, moved, back_sems.at[0]).wait()
     rows_wait(n_dir + 1, rows_send.at[0])
     scales_wait(n_dir - 1, scale_send.at[0])
-    pltpu.make_async_copy(rest, rest, ops_sems.at[2]).wait()
-    for sent in (ops_copy, list_copy, swap):
+    pltpu.make_async_copy(rest, rest, ops_sems.at[1]).wait()
+    mine = far_ops.at[:, pl.ds(0, deep + coarse_ops.shape[1] - shared_deep)]
+    pltpu.make_async_copy(mine, mine, ops_sems.at[0]).wait()
+    for sent in (list_copy, swap):
         sent.wait_send()
 
 
@@ -383,7 +389,7 @@
             pltpu.VMEM((dirs // 2, inside, coeffs), BF16),
             pltpu.VMEM((boxes, coeffs), F32),
             pltpu.SemaphoreType.DMA((9,)),
-        ] + [pltpu.SemaphoreType.DMA((n,)) for n in (1, 3, 1, 3, 1, 2, 4, 2, 3)],
+        ] + [pltpu.SemaphoreType.DMA((n,)) for n in (1, 3, 1, 3, 1, 2, 5, 2, 3)],
         compiler_params=pltpu.CompilerParams(
             collective_id=0, has_side_effects=True, vmem_limit_bytes=limit),
         name="translations",

time: 21.4 us -> 21.1 us (0.986)
  Pallas kernels: 20.6 us -> 20.3 us
    pallas_call x1, Pallas kernels: 19.8 us -> 19.5 us  [per_device(): pl.pallas_call(functools.partial(kernel, n_dir, n_space, boxes, dirs, blo...]
where the time goes in v4:
time: 21.1 us; the launch traced here: 20.9 us
  Pallas kernels  20.3 us (96%)
  between operations  0.64 us (3%)
    pallas_call x1, Pallas kernels, per_device(): pl.pallas_call(functools.partial(kernel, n_dir, n_space, boxes, dirs, blo...  19.5 us
    pallas_call x1, Pallas kernels, per_device(): pl.pallas_call(settle, out_shape=tuple((jax.ShapeDtypeStruct(out.shape, o...  0.82 us

profile of v4, /device:TPU:0, one launch (start us, length us, event | category | flops | bytes accessed | tf_op | source)
XLA Modules:
  0.0 20.9 jit_solution(14955217283836964688)
XLA Ops:
  0.6 19.5 %translations.1 = (f32[64,256]{1,0:T(8,128)S(1)}, bf16[16,64,256]{2,1,0:T(8,128)(2,1)S(1)}) custom-call(bf16[64,256]{1,0:T(8,128)(2,1)} %mult.1, f32[1,64]{1,0:T(1,128)} %bitcast.8, s32[2,4,512]{2,1,0:T(4,128)} %bitcast.5, s32[32,64]{1,0:T(8,128)} %bitcast.6, s32[32,64]{1,0:T(8,128)} %bitcast.7, s32[1,64]{1,0:T(1,128)} %bitcast.9, f32[16,128]{1,0:T(8,128)} %phases.1, ...), custom_call_target="tpu_custom_call" | custom-call | tf_op jit(solution)/shard_map/translations/pallas_call | solution.py:360
  20.1 0.8 %settle.1 = (f32[64,256]{1,0:T(8,128)}, bf16[16,64,256]{2,1,0:T(8,128)(2,1)}) custom-call(f32[64,256]{1,0:T(8,128)S(1)} %get-tuple-element.4.fine_in, bf16[16,64,256]{2,1,0:T(8,128)(2,1)S(1)} %get-tuple-element.5.coarse_in), custom_call_target="tpu_custom_call" | custom-call | tf_op jit(solution)/shard_map/settle/pallas_call | solution.py:402

commit v5 on v4

--- a/solution.py
+++ b/solution.py
@@ -51,7 +51,7 @@
            cand, scales, lists_v, far_lists, fine_v, wedge_v, count_v, slots_v, phases_v, fine_ops_v, coarse_ops_v, far_ops,
            columns, counts, weights, turns, rotated, sums, translated, gathered_out, gathered_in, fine_v_out,
            local_sem, rows_send, rows_recv, scale_send, scale_recv, halo_recv, list_sems, ops_sems,
-           swap_sems, back_sems):
+           back_sems):
     me = lax.axis_index("dir")
     space = lax.axis_index("space")
     group = n_dir * boxes
@@ -162,7 +162,7 @@
     list_copy.start()
     ops_copies = [pltpu.make_async_remote_copy(
         coarse_ops_v.at[share, rows], far_ops.at[:, rows],
-        ops_sems.at[0], ops_sems.at[3 + at], device_id={"dir": far}, device_id_type=MESH)
+        rows_send.at[0], ops_sems.at[1 + at], device_id={"dir": far}, device_id_type=MESH)
         for at, rows in enumerate((passed, common))]
 
     pulls[0].wait()
@@ -257,7 +257,7 @@
     ops_copies[0].wait_recv()
     for other in storeys:
         pltpu.make_async_remote_copy(
-            far_ops.at[:, passed], far_ops.at[:, passed], ops_sems.at[1], ops_sems.at[2],
+            far_ops.at[:, passed], far_ops.at[:, passed], rows_send.at[0], ops_sems.at[0],
             device_id={"space": other}, device_id_type=MESH).start()
     rows_wait(half - 1, rows_recv.at[2])
     for k in range(half + 1, n_dir):
@@ -277,9 +277,9 @@
             if k or not home:
                 where = {"dir": to} if home else {"dir": to, "space": sibling}
                 pltpu.make_async_remote_copy(
-                    piece, here, back_sems.at[0], back_sems.at[1], device_id=where, device_id_type=MESH).start()
+                    piece, here, rows_send.at[0], back_sems.at[0], device_id=where, device_id_type=MESH).start()
             else:
-                pltpu.make_async_copy(piece, here, back_sems.at[2]).start()
+                pltpu.make_async_copy(piece, here, back_sems.at[1]).start()
 
     def far_out(i):
         return coarse_out.at[far * dirs + core * share_dirs + i]
@@ -289,12 +289,12 @@
     for i in range(share_dirs):
         gathered_out[i] = gather(dirs + (1 - core) * share_dirs + i)
     swap = pltpu.make_async_remote_copy(
-        gathered_out, gathered_in, swap_sems.at[0], swap_sems.at[1],
+        gathered_out, gathered_in, rows_send.at[0], ops_sems.at[3],
         device_id={"space": sibling}, device_id_type=MESH)
     swap.start()
     own_gathered = [gather(dirs + core * share_dirs + i) for i in range(share_dirs)]
     rest = far_ops.at[:, pl.ds(0, (levels - 1) * deep)]
-    pltpu.make_async_copy(rest, rest, ops_sems.at[2]).wait()
+    pltpu.make_async_copy(rest, rest, ops_sems.at[0]).wait()
     ops_copies[1].wait_recv()
     for i in range(share_dirs):
         translate(own_gathered[i], far_ops[i], dirs + i, far_out(i), True)
@@ -317,17 +317,17 @@
 
     fine_copy.wait()
     kept = translated.at[pl.ds(0, dirs + share_dirs)]
-    pltpu.make_async_copy(kept, kept, back_sems.at[2]).wait()
-    moved = translated.at[pl.ds(0, 2 * dirs * half - dirs - share_dirs)]
-    pltpu.make_async_copy(moved, moved, back_sems.at[1]).wait()
+    pltpu.make_async_copy(kept, kept, back_sems.at[1]).wait()
+    returned = 2 * dirs * half - dirs - share_dirs
+    moved = translated.at[pl.ds(0, returned)]
     pltpu.make_async_copy(moved, moved, back_sems.at[0]).wait()
-    rows_wait(n_dir + 1, rows_send.at[0])
+    sent_rows = (
+        (n_dir + 1 + returned) * boxes
+        + share_dirs * (inside + levels * deep + coarse_ops.shape[1] - shared_deep))
+    sent = rotated.at[:, pl.ds(0, sent_rows // (2 * dirs))]
+    pltpu.make_async_copy(sent, sent, rows_send.at[0]).wait()
     scales_wait(n_dir - 1, scale_send.at[0])
-    pltpu.make_async_copy(rest, rest, ops_sems.at[1]).wait()
-    mine = far_ops.at[:, pl.ds(0, deep + coarse_ops.shape[1] - shared_deep)]
-    pltpu.make_async_copy(mine, mine, ops_sems.at[0]).wait()
-    for sent in (list_copy, swap):
-        sent.wait_send()
+    list_copy.wait_send()
 
 
 def settle(fine_in, coarse_in, fine_out, coarse_out, sems):
@@ -389,7 +389,7 @@
             pltpu.VMEM((dirs // 2, inside, coeffs), BF16),
             pltpu.VMEM((boxes, coeffs), F32),
             pltpu.SemaphoreType.DMA((9,)),
-        ] + [pltpu.SemaphoreType.DMA((n,)) for n in (1, 3, 1, 3, 1, 2, 5, 2, 3)],
+        ] + [pltpu.SemaphoreType.DMA((n,)) for n in (1, 3, 1, 3, 1, 2, 4, 2)],
         compiler_params=pltpu.CompilerParams(
             collective_id=0, has_side_effects=True, vmem_limit_bytes=limit),
         name="translations",

time: 21.1 us -> 21.1 us (level)
  no operation moved by 1% of the time
where the time goes in v5:
time: 21.1 us; the launch traced here: 20.9 us
  Pallas kernels  20.3 us (96%)
  between operations  0.64 us (3%)
    pallas_call x1, Pallas kernels, per_device(): pl.pallas_call(functools.partial(kernel, n_dir, n_space, boxes, dirs, blo...  19.4 us
    pallas_call x1, Pallas kernels, per_device(): pl.pallas_call(settle, out_shape=tuple((jax.ShapeDtypeStruct(out.shape, o...  0.82 us

profile of v5, /device:TPU:0, one launch (start us, length us, event | category | flops | bytes accessed | tf_op | source)
XLA Modules:
  0.0 20.9 jit_solution(5099582768210390990)
XLA Ops:
  0.6 19.4 %translations.1 = (f32[64,256]{1,0:T(8,128)S(1)}, bf16[16,64,256]{2,1,0:T(8,128)(2,1)S(1)}) custom-call(bf16[64,256]{1,0:T(8,128)(2,1)} %mult.1, f32[1,64]{1,0:T(1,128)} %bitcast.8, s32[2,4,512]{2,1,0:T(4,128)} %bitcast.5, s32[32,64]{1,0:T(8,128)} %bitcast.6, s32[32,64]{1,0:T(8,128)} %bitcast.7, s32[1,64]{1,0:T(1,128)} %bitcast.9, f32[16,128]{1,0:T(8,128)} %phases.1, ...), custom_call_target="tpu_custom_call" | custom-call | tf_op jit(solution)/shard_map/translations/pallas_call | solution.py:360
  20.1 0.8 %settle.1 = (f32[64,256]{1,0:T(8,128)}, bf16[16,64,256]{2,1,0:T(8,128)(2,1)}) custom-call(f32[64,256]{1,0:T(8,128)S(1)} %get-tuple-element.4.fine_in, bf16[16,64,256]{2,1,0:T(8,128)(2,1)S(1)} %get-tuple-element.5.coarse_in), custom_call_target="tpu_custom_call" | custom-call | tf_op jit(solution)/shard_map/settle/pallas_call | solution.py:402

commit v6 on v5

--- a/solution.py
+++ b/solution.py
@@ -82,10 +82,8 @@
     barrier = pltpu.get_barrier_semaphore()
     for k in range(1, half + 1):
         pl.semaphore_signal(barrier, inc=1, device_id={"dir": partner(me, k)}, device_id_type=MESH)
-    for k in range(1, half):
-        pl.semaphore_signal(
-            barrier, inc=1, device_id={"dir": partner(me, k), "space": sibling}, device_id_type=MESH)
-    for other in [above, below] + storeys:
+    greeted = [above, below] + (storeys if levels > 2 else [])
+    for other in greeted:
         pl.semaphore_signal(barrier, inc=1, device_id={"space": other}, device_id_type=MESH)
 
     pulls = [
@@ -121,7 +119,7 @@
 
         lax.fori_loop(0, half, count_rows, 0)
 
-    pl.semaphore_wait(barrier, 2 * half + levels)
+    pl.semaphore_wait(barrier, half + len(greeted))
 
     def rows_of(source):
         return pl.ds(pl.multiple_of(source * boxes, boxes), boxes)
@@ -254,6 +252,7 @@
     scales_wait(half - 1, scale_recv.at[2])
     for k in range(half + 1, n_dir):
         angles(partner(me, k))
+    rows_wait(2, halo_recv.at[0])
     ops_copies[0].wait_recv()
     for other in storeys:
         pltpu.make_async_remote_copy(
@@ -302,7 +301,6 @@
     for i in range(share_dirs):
         translate(gathered_in[i], far_ops[i], dirs + share_dirs + i, far_out(i), False)
 
-    rows_wait(2, halo_recv.at[0])
     for g in range(blocks):
         total = jnp.dot(weights[g * members:(g + 1) * members, :], cand[...], preferred_element_type=F32).astype(BF16)
         for w in range(wedges):

time: 21.1 us -> 20.9 us (level)
  no operation moved by 1% of the time
where the time goes in v6:
time: 20.9 us; the launch traced here: 20.7 us
  Pallas kernels  20.1 us (96%)
  between operations  0.64 us (3%)
    pallas_call x1, Pallas kernels, per_device(): pl.pallas_call(functools.partial(kernel, n_dir, n_space, boxes, dirs, blo...  19.3 us
    pallas_call x1, Pallas kernels, per_device(): pl.pallas_call(settle, out_shape=tuple((jax.ShapeDtypeStruct(out.shape, o...  0.82 us

profile of v6, /device:TPU:0, one launch (start us, length us, event | category | flops | bytes accessed | tf_op | source)
XLA Modules:
  0.0 20.7 jit_solution(5153606182313515086)
XLA Ops:
  0.6 19.3 %translations.1 = (f32[64,256]{1,0:T(8,128)S(1)}, bf16[16,64,256]{2,1,0:T(8,128)(2,1)S(1)}) custom-call(bf16[64,256]{1,0:T(8,128)(2,1)} %mult.1, f32[1,64]{1,0:T(1,128)} %bitcast.8, s32[2,4,512]{2,1,0:T(4,128)} %bitcast.5, s32[32,64]{1,0:T(8,128)} %bitcast.6, s32[32,64]{1,0:T(8,128)} %bitcast.7, s32[1,64]{1,0:T(1,128)} %bitcast.9, f32[16,128]{1,0:T(8,128)} %phases.1, ...), custom_call_target="tpu_custom_call" | custom-call | tf_op jit(solution)/shard_map/translations/pallas_call | solution.py:358
  19.9 0.8 %settle.1 = (f32[64,256]{1,0:T(8,128)}, bf16[16,64,256]{2,1,0:T(8,128)(2,1)}) custom-call(f32[64,256]{1,0:T(8,128)S(1)} %get-tuple-element.4.fine_in, bf16[16,64,256]{2,1,0:T(8,128)(2,1)S(1)} %get-tuple-element.5.coarse_in), custom_call_target="tpu_custom_call" | custom-call | tf_op jit(solution)/shard_map/settle/pallas_call | solution.py:400

commit v7 on v6

--- a/solution.py
+++ b/solution.py
@@ -48,7 +48,7 @@
 def kernel(n_dir, n_space, boxes, dirs, block_boxes, mult, scale, lists, fine_list, wedge_index, list_count, phases,
            fine_ops, coarse_ops,
            fine_out, coarse_out,
-           cand, scales, lists_v, far_lists, fine_v, wedge_v, count_v, slots_v, phases_v, fine_ops_v, coarse_ops_v, far_ops,
+           cand, scales, lists_v, far_lists, pairs_v, count_v, slots_v, phases_v, fine_ops_v, coarse_ops_v, far_ops,
            columns, counts, weights, turns, rotated, sums, translated, gathered_out, gathered_in, fine_v_out,
            local_sem, rows_send, rows_recv, scale_send, scale_recv, halo_recv, list_sems, ops_sems,
            back_sems):
@@ -88,14 +88,14 @@
 
     pulls = [
         pltpu.make_async_copy(lists.at[:, :, pl.ds(first_inside, inside)], lists_v, local_sem.at[0]),
-        pltpu.make_async_copy(fine_list, fine_v, local_sem.at[1]),
-        pltpu.make_async_copy(wedge_index, wedge_v, local_sem.at[2]),
+        pltpu.make_async_copy(fine_list, pairs_v.at[0], local_sem.at[1]),
+        pltpu.make_async_copy(wedge_index, pairs_v.at[1], local_sem.at[1]),
         pltpu.make_async_copy(mult, cand.at[own], local_sem.at[3]),
         pltpu.make_async_copy(scale, scales.at[me], local_sem.at[4]),
         pltpu.make_async_copy(phases, phases_v, local_sem.at[5]),
         pltpu.make_async_copy(coarse_ops, coarse_ops_v, local_sem.at[6]),
         pltpu.make_async_copy(fine_ops, fine_ops_v, local_sem.at[7]),
-        pltpu.make_async_copy(list_count, count_v, local_sem.at[8]),
+        pltpu.make_async_copy(list_count, count_v, local_sem.at[2]),
     ]
     for at in (3, 4, 0, 6, 1, 2, 8, 5, 7):
         pulls[at].start()
@@ -152,7 +152,7 @@
         send_rows(k, k, cand.at[own], me)
     for side, other in ((0, above), (1, below)):
         pltpu.make_async_remote_copy(
-            mult, cand.at[pl.ds(group + side * boxes, boxes)], rows_send.at[0], halo_recv.at[0],
+            cand.at[own], cand.at[pl.ds(group + side * boxes, boxes)], rows_send.at[0], halo_recv.at[0],
             device_id={"space": other}, device_id_type=MESH).start()
     list_copy = pltpu.make_async_remote_copy(
         lists.at[:, :, pl.ds(first_far, inside)], far_lists, list_sems.at[0], list_sems.at[1],
@@ -168,18 +168,17 @@
     set_counts(0)
     pulls[6].wait()
 
-    pulls[1].wait()
-    pulls[2].wait()
+    pltpu.make_async_copy(pairs_v, pairs_v, local_sem.at[1]).wait()
     pulls[8].wait()
     blocks = boxes // block_boxes
     members = block_boxes * wedges
-    width_list = fine_v.shape[0]
-    first = fine_v[...] - space * group
+    width_list = pairs_v.shape[1]
+    first = pairs_v[0] - space * group
     slot_values = jnp.where(
         first < 0, first + (2 * group - me * boxes), jnp.where(first < group, first, first + (boxes - me * boxes)))
     box = lax.broadcasted_iota(jnp.int32, (width_list, boxes), 1)
     term = lax.broadcasted_iota(jnp.int32, (width_list, boxes), 0)
-    code_values = jnp.where(term < count_v[...], wedge_v[...] * block_boxes + box % block_boxes, -1)
+    code_values = jnp.where(term < count_v[...], pairs_v[1] * block_boxes + box % block_boxes, -1)
     packs = LANES // block_boxes
     depth = width_list // packs
     blank = jnp.zeros((width_list, LANES - boxes), jnp.int32)
@@ -278,7 +277,7 @@
                 pltpu.make_async_remote_copy(
                     piece, here, rows_send.at[0], back_sems.at[0], device_id=where, device_id_type=MESH).start()
             else:
-                pltpu.make_async_copy(piece, here, back_sems.at[1]).start()
+                pltpu.make_async_copy(piece, here, local_sem.at[1]).start()
 
     def far_out(i):
         return coarse_out.at[far * dirs + core * share_dirs + i]
@@ -315,7 +314,7 @@
 
     fine_copy.wait()
     kept = translated.at[pl.ds(0, dirs + share_dirs)]
-    pltpu.make_async_copy(kept, kept, back_sems.at[1]).wait()
+    pltpu.make_async_copy(kept, kept, local_sem.at[1]).wait()
     returned = 2 * dirs * half - dirs - share_dirs
     moved = translated.at[pl.ds(0, returned)]
     pltpu.make_async_copy(moved, moved, back_sems.at[0]).wait()
@@ -368,8 +367,7 @@
             pltpu.VMEM((n_dir, 1, boxes), F32),
             pltpu.VMEM((dirs, terms, inside), jnp.int32),
             pltpu.VMEM((dirs, terms, inside), jnp.int32),
-            pltpu.VMEM((list_width, boxes), jnp.int32),
-            pltpu.VMEM((list_width, boxes), jnp.int32),
+            pltpu.VMEM((2, list_width, boxes), jnp.int32),
             pltpu.VMEM((1, boxes), jnp.int32),
             pltpu.VMEM((2, list_width, LANES), jnp.int32),
             pltpu.VMEM(phases.shape, F32),
@@ -386,8 +384,8 @@
             pltpu.VMEM((dirs // 2, inside, coeffs), BF16),
             pltpu.VMEM((dirs // 2, inside, coeffs), BF16),
             pltpu.VMEM((boxes, coeffs), F32),
-            pltpu.SemaphoreType.DMA((9,)),
-        ] + [pltpu.SemaphoreType.DMA((n,)) for n in (1, 3, 1, 3, 1, 2, 4, 2)],
+            pltpu.SemaphoreType.DMA((8,)),
+        ] + [pltpu.SemaphoreType.DMA((n,)) for n in (1, 3, 1, 3, 1, 2, 4, 1)],
         compiler_params=pltpu.CompilerParams(
             collective_id=0, has_side_effects=True, vmem_limit_bytes=limit),
         name="translations",

time: 20.9 us -> 20.9 us (level)
  no operation moved by 1% of the time
where the time goes in v7:
time: 20.9 us; the launch traced here: 20.7 us
  Pallas kernels  20.1 us (96%)
  between operations  0.64 us (3%)
    pallas_call x1, Pallas kernels, per_device(): pl.pallas_call(functools.partial(kernel, n_dir, n_space, boxes, dirs, blo...  19.2 us
    pallas_call x1, Pallas kernels, per_device(): pl.pallas_call(settle, out_shape=tuple((jax.ShapeDtypeStruct(out.shape, o...  0.82 us

profile of v7, /device:TPU:0, one launch (start us, length us, event | category | flops | bytes accessed | tf_op | source)
XLA Modules:
  0.0 20.7 jit_solution(2926186790575374312)
XLA Ops:
  0.6 19.2 %translations.1 = (f32[64,256]{1,0:T(8,128)S(1)}, bf16[16,64,256]{2,1,0:T(8,128)(2,1)S(1)}) custom-call(bf16[64,256]{1,0:T(8,128)(2,1)} %mult.1, f32[1,64]{1,0:T(1,128)} %bitcast.8, s32[2,4,512]{2,1,0:T(4,128)} %bitcast.5, s32[32,64]{1,0:T(8,128)} %bitcast.6, s32[32,64]{1,0:T(8,128)} %bitcast.7, s32[1,64]{1,0:T(1,128)} %bitcast.9, f32[16,128]{1,0:T(8,128)} %phases.1, ...), custom_call_target="tpu_custom_call" | custom-call | tf_op jit(solution)/shard_map/translations/pallas_call | solution.py:357
  19.9 0.8 %settle.1 = (f32[64,256]{1,0:T(8,128)}, bf16[16,64,256]{2,1,0:T(8,128)(2,1)}) custom-call(f32[64,256]{1,0:T(8,128)S(1)} %get-tuple-element.4.fine_in, bf16[16,64,256]{2,1,0:T(8,128)(2,1)S(1)} %get-tuple-element.5.coarse_in), custom_call_target="tpu_custom_call" | custom-call | tf_op jit(solution)/shard_map/settle/pallas_call | solution.py:398
